TPU v7x, 32 devices: a whole 2x2x4 slice. The times are simulated.
32 devices in a mesh: dp: 16 (over z, x, core), shard: 2 (over y).
Axes of the slice: x: 2, y: 2, z: 4, core: 2. Of those that a mesh axis runs over, the one named last changes fastest.
Arguments:
- tokens: bfloat16 [4096, 1088], P(('dp', 'shard')), may hold values from -6 to 6
- seq_ends: int32 [32, 3], P(('dp', 'shard')), may hold values from 0 to 128, as said below
- attn_weight: bfloat16 [1, 4352, 1088], P(None, ('dp', 'shard'))
- up_weight: bfloat16 [1, 4352, 1088], P(None, ('dp', 'shard')), may hold values from -0.1875 to 0.1875
- down_weight: bfloat16 [1, 4352, 1088], P(None, ('dp', 'shard')), may hold values from -0.09375 to 0.09375
- vectors: bfloat16 [1, 13056], P(None, ('dp', 'shard'))
- cotangent: bfloat16 [4096, 1088], P(('dp', 'shard')), may hold values from -6 to 6
Outputs:
- output: bfloat16 [4096, 1088], P(('dp', 'shard'))
- grad_tokens: float32 [4096, 1088], P(('dp', 'shard'))
- grad_attn: float32 [1, 4352, 1088], P(None, ('dp', 'shard'))
- grad_up: float32 [1, 4352, 1088], P(None, ('dp', 'shard'))
- grad_down: float32 [1, 4352, 1088], P(None, ('dp', 'shard'))
- grad_vectors: float32 [1, 13056], P(None, ('dp', 'shard'))
Inputs may be any that keep to these rules, and one draw needn't show every extreme that they name: `seq_ends`: each row lists non-decreasing end offsets of the sequences packed into one device's 128 slots; slots from the row's last end onward form one more segment.
All inputs are finite; a program needn't handle non-finite values.
Results may differ from a plain program's by a relative error of at most 0.0089.
Values may be sent and summed in bfloat16 or wider, within the bound.
A program may use at most 192 MiB of HBM per device.

v0:
```python
import jax
import jax.numpy as jnp
from jax import lax
from jax.sharding import PartitionSpec as P

HEAD_DIM = 64
EPS = 1e-05


def layer_norm(values, gain, shift):
    average = jnp.mean(values, axis=-1, keepdims=True)
    centred = values - average
    variance = jnp.mean(centred * centred, axis=-1, keepdims=True)
    return centred * lax.rsqrt(variance + EPS) * gain + shift


def gelu_tanh(values):
    return (
        0.5
        * values
        * (1.0 + jnp.tanh(0.7978845608028654 * (values + 0.044715 * values * values * values)))
    )


def contract_last(left, right):
    return lax.dot_general(
        left, right, (((1,), (1,)), ((), ())), preferred_element_type=jnp.float32
    )


def contract_first(left, right):
    return lax.dot_general(
        left, right, (((0,), (0,)), ((), ())), preferred_element_type=jnp.float32
    )


def head_product(form, left, right):
    return jnp.einsum(form, left, right, preferred_element_type=jnp.float32)


def causal_mask(ends_row, slot_count):
    positions = jnp.arange(slot_count, dtype=jnp.int32)
    segment = jnp.sum((ends_row[None, :] <= positions[:, None]).astype(jnp.int32), axis=1)
    return (segment[:, None] == segment[None, :]) & (positions[None, :] <= positions[:, None])


def split_vectors(vectors, model_width):
    vector_f32 = vectors.astype(jnp.float32)
    parts_list = [
        vector_f32[slot_idx * model_width : (slot_idx + 1) * model_width] for slot_idx in range(8)
    ]
    return parts_list + [vector_f32[8 * model_width :]]


def forward_layer(hidden, params, allowed):
    attn_part, up_part, down_part, vector_part = params
    model_width = attn_part.shape[1]
    head_count = model_width // HEAD_DIM
    row_count = hidden.shape[0]
    (
        gain_one,
        shift_one,
        query_bias,
        value_bias,
        out_bias,
        gain_two,
        shift_two,
        down_bias,
        up_bias,
    ) = split_vectors(vector_part, model_width)
    normed_one = layer_norm(hidden, gain_one, shift_one).astype(jnp.bfloat16)
    projected = contract_last(normed_one, attn_part[: 3 * model_width])
    query_heads = (
        ((projected[:, :model_width] + query_bias) * HEAD_DIM ** (-0.5))
        .astype(jnp.bfloat16)
        .reshape(row_count, head_count, HEAD_DIM)
    )
    key_heads = (
        projected[:, model_width : 2 * model_width]
        .astype(jnp.bfloat16)
        .reshape(row_count, head_count, HEAD_DIM)
    )
    value_heads = (
        (projected[:, 2 * model_width :] + value_bias)
        .astype(jnp.bfloat16)
        .reshape(row_count, head_count, HEAD_DIM)
    )
    scores = jnp.where(allowed[None], head_product("qhc,khc->hqk", query_heads, key_heads), -1e30)
    log_total = jnp.log(jnp.sum(jnp.exp(scores), axis=-1))
    weights = jnp.exp(scores - log_total[..., None]).astype(jnp.bfloat16)
    context = (
        head_product("hqk,khc->qhc", weights, value_heads)
        .reshape(row_count, model_width)
        .astype(jnp.bfloat16)
    )
    after_attn = (
        hidden
        + jnp.dot(context, attn_part[3 * model_width :], preferred_element_type=jnp.float32)
        + out_bias
    )
    normed_two = layer_norm(after_attn, gain_two, shift_two).astype(jnp.bfloat16)
    pre_act = contract_last(normed_two, up_part) + up_bias
    activated = gelu_tanh(pre_act).astype(jnp.bfloat16)
    result = (
        after_attn + jnp.dot(activated, down_part, preferred_element_type=jnp.float32) + down_bias
    )
    saved_acts = (
        hidden,
        normed_one,
        query_heads,
        key_heads,
        value_heads,
        log_total,
        context,
        after_attn,
        normed_two,
        pre_act,
        activated,
    )
    return (result, saved_acts)


def backward_layer(upstream, params, saved_acts, allowed):
    attn_part, up_part, down_part, vector_part = params
    (
        hidden,
        normed_one,
        query_heads,
        key_heads,
        value_heads,
        log_total,
        context,
        after_attn,
        normed_two,
        pre_act,
        activated,
    ) = saved_acts
    model_width = attn_part.shape[1]
    head_count = model_width // HEAD_DIM
    row_count = hidden.shape[0]
    (
        gain_one,
        shift_one,
        query_bias,
        value_bias,
        out_bias,
        gain_two,
        shift_two,
        down_bias,
        up_bias,
    ) = split_vectors(vector_part, model_width)
    upstream_bf = upstream.astype(jnp.bfloat16)
    grad_down_bias = jnp.sum(upstream, axis=0)
    grad_act = contract_last(upstream_bf, down_part)
    grad_pre = jax.vjp(gelu_tanh, pre_act)[1](grad_act)[0]
    grad_up_bias = jnp.sum(grad_pre, axis=0)
    grad_pre_bf = grad_pre.astype(jnp.bfloat16)
    grad_normed_two = jnp.dot(grad_pre_bf, up_part, preferred_element_type=jnp.float32)
    back_two = jax.vjp(layer_norm, after_attn, gain_two, shift_two)[1]
    grad_mid, grad_gain_two, grad_shift_two = back_two(grad_normed_two)
    grad_mid = upstream + grad_mid
    grad_out_bias = jnp.sum(grad_mid, axis=0)
    grad_mid_bf = grad_mid.astype(jnp.bfloat16)
    grad_context = (
        contract_last(grad_mid_bf, attn_part[3 * model_width :])
        .astype(jnp.bfloat16)
        .reshape(row_count, head_count, HEAD_DIM)
    )
    scores = jnp.where(allowed[None], head_product("qhc,khc->hqk", query_heads, key_heads), -1e30)
    probs_f32 = jnp.exp(scores - log_total[..., None])
    probs_bf = probs_f32.astype(jnp.bfloat16)
    grad_values = head_product("hqk,qhc->khc", probs_bf, grad_context).reshape(
        row_count, model_width
    )
    grad_probs = head_product("qhc,khc->hqk", grad_context, value_heads)
    row_dot = jnp.sum(probs_f32 * grad_probs, axis=-1, keepdims=True)
    grad_scores = (probs_f32 * (grad_probs - row_dot)).astype(jnp.bfloat16)
    grad_query = head_product("hqk,khc->qhc", grad_scores, key_heads).reshape(
        row_count, model_width
    ) * HEAD_DIM ** (-0.5)
    grad_keys = head_product("hqk,qhc->khc", grad_scores, query_heads).reshape(
        row_count, model_width
    )
    grad_query_bias = jnp.sum(grad_query, axis=0)
    grad_value_bias = jnp.sum(grad_values, axis=0)
    grad_proj = jnp.concatenate([grad_query, grad_keys, grad_values], axis=1).astype(jnp.bfloat16)
    grad_normed_one = jnp.dot(
        grad_proj, attn_part[: 3 * model_width], preferred_element_type=jnp.float32
    )
    back_one = jax.vjp(layer_norm, hidden, gain_one, shift_one)[1]
    grad_below, grad_gain_one, grad_shift_one = back_one(grad_normed_one)
    grad_below = grad_mid + grad_below
    left_all = jnp.concatenate([grad_proj, context], axis=1)
    grad_vector = jnp.concatenate(
        [
            grad_gain_one,
            grad_shift_one,
            grad_query_bias,
            grad_value_bias,
            grad_out_bias,
            grad_gain_two,
            grad_shift_two,
            grad_down_bias,
            grad_up_bias,
        ]
    )
    operands = (left_all, normed_one, grad_mid_bf, grad_pre_bf, normed_two, activated, upstream_bf)
    return (grad_below, operands, grad_vector)


def shards(tokens, seq_ends, attn_weight, up_weight, down_weight, vectors, cotangent):
    allowed = causal_mask(seq_ends[0], tokens.shape[0])
    model_width = tokens.shape[1]
    attn_rows = attn_weight.shape[1]
    layer_count = attn_weight.shape[0]
    hidden = tokens.astype(jnp.float32)
    kept_params = []
    layer_idx = 0
    gathered = (
        lax.all_gather(attn_weight[layer_idx], ("dp", "shard"), axis=0, tiled=True),
        lax.all_gather(up_weight[layer_idx], ("dp", "shard"), axis=0, tiled=True),
        lax.all_gather(down_weight[layer_idx], ("dp", "shard"), axis=0, tiled=True),
        lax.all_gather(vectors[layer_idx], ("dp", "shard"), axis=0, tiled=True),
    )
    kept_params.append(gathered)
    hidden, saved_acts = forward_layer(hidden, gathered, allowed)
    saved_list = [saved_acts]
    output = hidden.astype(jnp.bfloat16)
    upstream = cotangent.astype(jnp.float32)
    grad_sets = [None] * layer_count
    for layer_idx in reversed(range(layer_count)):
        gathered = (
            lax.all_gather(attn_weight[layer_idx], ("dp", "shard"), axis=0, tiled=True),
            lax.all_gather(up_weight[layer_idx], ("dp", "shard"), axis=0, tiled=True),
            lax.all_gather(down_weight[layer_idx], ("dp", "shard"), axis=0, tiled=True),
            lax.all_gather(vectors[layer_idx], ("dp", "shard"), axis=0, tiled=True),
        )
        upstream, operands, grad_vector = backward_layer(
            upstream, gathered, saved_list[layer_idx], allowed
        )
        left_all, normed_one, grad_mid_bf, grad_pre_bf, normed_two, activated, upstream_bf = (
            operands
        )
        row_index = jnp.arange(attn_rows * lax.axis_size(("dp", "shard")), dtype=jnp.int32)
        first_rows = jnp.where(
            (row_index < 3 * model_width)[None, :], left_all, jnp.zeros_like(left_all)
        )
        second_rows = jnp.where(
            (row_index >= 3 * model_width)[None, :], left_all, jnp.zeros_like(left_all)
        )
        grad_attn_w = lax.psum_scatter(
            contract_first(first_rows, normed_one) + contract_first(second_rows, grad_mid_bf),
            ("dp", "shard"),
            scatter_dimension=0,
            tiled=True,
        )
        grad_up_w = lax.psum_scatter(
            contract_first(grad_pre_bf, normed_two),
            ("dp", "shard"),
            scatter_dimension=0,
            tiled=True,
        )
        grad_down_w = lax.psum_scatter(
            contract_first(activated, upstream_bf), ("dp", "shard"), scatter_dimension=0, tiled=True
        )
        grad_vec_own = lax.psum_scatter(
            grad_vector, ("dp", "shard"), scatter_dimension=0, tiled=True
        )
        grad_sets[layer_idx] = (grad_attn_w, grad_up_w, grad_down_w, grad_vec_own)
    grad_attn = jnp.stack([grad_sets[0][0]])
    grad_up = jnp.stack([grad_sets[0][1]])
    grad_down = jnp.stack([grad_sets[0][2]])
    grad_vectors = jnp.stack([grad_sets[0][3]])
    return (output, upstream, grad_attn, grad_up, grad_down, grad_vectors)


def solution(mesh):
    return jax.shard_map(
        shards,
        mesh=mesh,
        in_specs=(
            P(("dp", "shard"), None),
            P(("dp", "shard"), None),
            P(None, ("dp", "shard"), None),
            P(None, ("dp", "shard"), None),
            P(None, ("dp", "shard"), None),
            P(None, ("dp", "shard")),
            P(("dp", "shard"), None),
        ),
        out_specs=(
            P(("dp", "shard"), None),
            P(("dp", "shard"), None),
            P(None, ("dp", "shard"), None),
            P(None, ("dp", "shard"), None),
            P(None, ("dp", "shard"), None),
            P(None, ("dp", "shard")),
        ),
        check_vma=False,
    )
```

profile of v0, /device:TPU:0, one launch (start us, length us, event | category | flops | bytes accessed | tf_op | source)
XLA Modules:
  0.0 987.9 jit_solution(13790586589980789792)
XLA Ops:
  7.2 0.7 all-gather.8.cloned.1.call-update
  7.9 0.7 all-gather.10.cloned.1.call-update
  8.7 0.7 all-gather.12.cloned.1.call-update
  9.4 0.7 reduce.3
  10.2 0.3 dynamic-update-slice
  10.4 43.7 %all-reduce = bf16[13056]{0:T(1024)(128)(2,1)S(1)} all-reduce(bf16[13056]{0:T(1024)(128)(2,1)S(1)} %dynamic-update-slice), channel_id=2, replica_groups=mesh['dp'=16,'shard'=2] {'dp','shard'}, use_global_device_ids=true, to_apply=%add | all-reduce | flops 13056 | bytes 52224
  54.2 0.7 convert_reduce_fusion.2
  55.0 0.1 slice_reduce_fusion.3
  55.1 1.1 convert_reduce_fusion
  56.2 1.1 fusion.54
  57.3 0.1 fusion.77
  57.4 40.9 %all-gather.8.cloned.1.call-done = bf16[1,4352,1088]{2,1,0:T(8,128)(2,1)} async-done(((bf16[1,136,1088]{2,1,0:T(8,128)(2,1)}), bf16[1,4352,1088]{2,1,0:T(8,128)(2,1)}) %all-gather.8.cloned.1.call-update) | async-done | bytes 9469968 | tf_op jit(solution)/shard_map/all_gather | solution.py:220
  98.4 5.4 fusion.10
  103.9 0.4 fusion.57
  104.3 0.4 convolution_select_fusion
  104.6 0.5 convolution_convert_fusion.2
  105.2 3.0 fusion.94
  108.1 0.2 multiply_reduce_fusion.3
  108.3 75.5 %all-gather.10.cloned.1.call-done = bf16[1,4352,1088]{2,1,0:T(8,128)(2,1)} async-done(((bf16[1,136,1088]{2,1,0:T(8,128)(2,1)}), bf16[1,4352,1088]{2,1,0:T(8,128)(2,1)}) %all-gather.10.cloned.1.call-update) | async-done | bytes 9469968 | tf_op jit(solution)/shard_map/all_gather | solution.py:221
  183.9 7.2 fusion.11
  191.1 78.3 %all-gather.12.cloned.1.call-done = bf16[1,4352,1088]{2,1,0:T(8,128)(2,1)} async-done(((bf16[1,136,1088]{2,1,0:T(8,128)(2,1)}), bf16[1,4352,1088]{2,1,0:T(8,128)(2,1)}) %all-gather.12.cloned.1.call-update) | async-done | bytes 9469968 | tf_op jit(solution)/shard_map/all_gather | solution.py:222
  269.4 7.4 fusion.97
  276.8 4.7 multiply_reduce_fusion.1
  281.6 0.2 fusion.91
  281.9 0.8 copy-done.2
  282.6 0.1 fusion.75
  282.8 3.3 convolution_convert_fusion
  286.1 3.0 fusion.92
  289.1 1.4 fusion.98
  290.5 1.3 multiply_reduce_fusion
  291.9 0.2 multiply_convert_fusion.1
  292.1 0.7 copy-done.9
  292.8 0.5 convolution_convert_fusion.1
  293.3 0.4 fusion.93
  293.7 14.5 %fusion.35 = f32[4352,1088]{1,0:T(8,128)} fusion(pred[4352]{0:T(1024)(128)(4,1)S(1)} %iota_compare_fusion.2, bf16[128,1088]{0,1:T(8,128)(2,1)S(1)} %bitcast.88, bf16[128,1088]{0,1:T(8,128)(2,1)S(1)} %bitcast.85, bf16[128,1088]{0,1:T(8,128)(2,1)S(1)} %bitcast.74, bf16[128,1088]{0,1:T(8,128)(2,1)S(1)} %bitcast.77, bf16[128,1088]{0,1:T(8,128)(2,1)S(1)} %copy-done.1, ...), kind=kOutput, calls=%fused_computation.41 | convolution fusion | flops 1218002944 | bytes 20346624 | tf_op jit(solution)/shard_map/dot_general | solution.py:32
  308.2 20.0 %convolution_add_fusion = f32[4352,1088]{1,0:T(8,128)} fusion(f32[4352,1088]{1,0:T(8,128)} %fusion.35, bf16[128,1088]{0,1:T(8,128)(2,1)S(1)} %copy-done.18, pred[4352]{0:T(1024)(128)(4,1)S(1)} %iota_compare_fusion.1, bf16[128,1088]{0,1:T(8,128)(2,1)S(1)} %bitcast.89, bf16[128,1088]{0,1:T(8,128)(2,1)S(1)} %bitcast.86, bf16[128,1088]{0,1:T(8,128)(2,1)S(1)} %bitcast.75, ...), kind=kOutput, calls=%fused_computation.1 | convolution fusion | flops 1221902336 | bytes 39276800 | tf_op jit(solution)/shard_map/dot_general | solution.py:32
  328.2 12.6 %fusion.61 = f32[4352,1088]{1,0:T(8,128)} fusion(bf16[128,4352]{1,0:T(8,128)(2,1)} %copy-done.4, f32[128,1088]{0,1:T(8,128)S(1)} %get-tuple-element.33, f32[1088]{0:T(1024)S(1)} %get-tuple-element.16, f32[1088]{0:T(1024)S(1)} %get-tuple-element.15, f32[128]{0:T(128)S(1)} %fusion.81, f32[128]{0:T(128)S(1)} %broadcast_multiply_fusion), kind=kOutput, calls=%fused_computation.82 | convolution fusion | flops 1212850176 | bytes 20620800 | tf_op jit(solution)/shard_map/dot_general | solution.py:32
  340.9 11.0 %fusion.89 = f32[4352,1088]{1,0:T(8,128)} fusion(bf16[128,1088]{0,1:T(8,128)(2,1)} %param.13, f32[128,4352]{1,0:T(8,128)S(1)} %fusion.11), kind=kOutput, calls=%fused_computation.124 | convolution fusion | flops 1217167360 | bytes 21446656 | tf_op jit(solution)/shard_map/dot_general | solution.py:32
  352.1 7.2 fusion.90
  359.3 0.4 fusion.53
  359.8 1.2 convert_reduce_fusion.1
  361.0 0.1 concatenate.13
  361.1 40.9 %all-reduce.4 = f32[13056]{0:T(1024)S(1)} all-reduce(f32[13056]{0:T(1024)S(1)} %concatenate.13), channel_id=9, replica_groups=mesh['dp'=16,'shard'=2] {'dp','shard'}, use_global_device_ids=true, to_apply=%region_23.24.clone | all-reduce | flops 13056 | bytes 104448
  402.0 0.7 dynamic-slice.3
  402.6 8.3 fusion.21
  411.0 130.0 %reduce-scatter.10.cloned.1.call-done = f32[136,1088]{1,0:T(8,128)} async-done(((f32[4352,1088]{1,0:T(8,128)}), f32[136,1088]{1,0:T(8,128)}) %reduce-scatter.10.cloned.1.call-update) | async-done | bytes 591888
  540.9 219.9 %reduce-scatter.12.cloned.1.call-done = f32[136,1088]{1,0:T(8,128)} async-done(((f32[4352,1088]{1,0:T(8,128)}), f32[136,1088]{1,0:T(8,128)}) %reduce-scatter.12.cloned.1.call-update) | async-done | bytes 591888
  760.9 219.9 %reduce-scatter.14.cloned.1.call-done = f32[136,1088]{1,0:T(8,128)} async-done(((f32[4352,1088]{1,0:T(8,128)}), f32[136,1088]{1,0:T(8,128)}) %reduce-scatter.14.cloned.1.call-update) | async-done | bytes 591888
  (65 shorter events, 0.7 us)
Async XLA Ops:
  7.2 91.2 %all-gather.8.cloned.1.call-start = ((), (), s32[]{:S(2)}) async-start(), calls=%async_computation.3 | async-start | bytes 10340352 | tf_op jit(solution)/shard_map/all_gather | solution.py:220
  7.9 176.0 %all-gather.10.cloned.1.call-start = ((), (), s32[]{:S(2)}) async-start(), calls=%async_computation.4 | async-start | bytes 10340352 | tf_op jit(solution)/shard_map/all_gather | solution.py:221
  8.6 260.7 %all-gather.12.cloned.1.call-start = ((), (), s32[]{:S(2)}) async-start(), calls=%async_computation.5 | async-start | bytes 10340352 | tf_op jit(solution)/shard_map/all_gather | solution.py:222
  9.4 531.5 %reduce-scatter.10.cloned.1.call-start = ((), (), s32[]{:S(2)}) async-start(), calls=%async_computation.6 | async-start | bytes 20680704
  103.9 1.3 copy-start.10
  103.9 1.3 copy-start.1
  104.2 0.9 copy-start.8
  104.3 3.9 copy-start.19
  104.6 3.5 copy-start.5
  105.1 3.2 copy-start.15
  183.9 85.5 %copy-start.12 = (bf16[128,1088]{0,1:T(8,128)(2,1)S(1)}, bf16[128,1088]{0,1:T(8,128)(2,1)}, u32[]{:S(2)}) copy-start(bf16[128,1088]{0,1:T(8,128)(2,1)} %param.13) | copy-start | bytes 835588
  269.4 7.5 copy-start
  276.8 4.8 copy-start.4
  281.8 0.8 copy-start.2
  282.7 3.4 copy-start.17
  282.7 6.4 copy-start.20
  289.1 1.4 copy-start.6
  291.9 1.0 copy-start.9
  291.9 1.4 copy-start.11
  291.9 1.8 copy-start.14
  291.9 1.8 copy-start.16
  293.7 14.5 %copy-start.7 = (bf16[17,64,128]{2,1,0:T(8,128)(2,1)}, bf16[17,64,128]{2,1,0:T(8,128)(2,1)S(1)}, u32[]{:S(2)}) copy-start(bf16[17,64,128]{2,1,0:T(8,128)(2,1)S(1)} %get-tuple-element.31) | copy-start | bytes 835588
  293.7 14.5 %copy-start.18 = (bf16[128,1088]{0,1:T(8,128)(2,1)S(1)}, bf16[128,1088]{0,1:T(8,128)(2,1)}, u32[]{:S(2)}) copy-start(bf16[128,1088]{0,1:T(8,128)(2,1)} %copy-done.17) | copy-start | bytes 835588
  328.2 432.7 %reduce-scatter.12.cloned.1.call-start = ((), (), s32[]{:S(2)}) async-start(), calls=%async_computation.7 | async-start | bytes 20680704
  340.8 639.9 %reduce-scatter.14.cloned.1.call-start = ((), (), s32[]{:S(2)}) async-start(), calls=%async_computation.8 | async-start | bytes 20680704
  352.1 7.7 copy-start.3
  352.1 7.7 copy-start.13
Sparse Core Ops, SparseCore 0:
  10.8 87.5 all-gather.7
  101.2 82.5 all-gather.9
  186.7 82.5 all-gather.11
  328.3 212.5 reduce-scatter.9
  547.8 213.0 reduce-scatter.11
  767.7 213.0 reduce-scatter.13
where the time goes:
time: 998 us; the launch traced here: 988 us
  waiting for transfers between devices  767 us (77%)
  matrix products  111 us (11%)
  blocking collectives  84.6 us (8%)
  between operations  14.8 us (1%)
    unnamed x9, waiting for transfers between devices  572 us
    unnamed x2, blocking collectives  84.6 us
    all_gather x1, waiting for transfers between devices, shards(): lax.all_gather(down_weight[layer_idx], ('dp', 'shard'), axis=0, tiled=True)  78.3 us
    all_gather x1, waiting for transfers between devices, shards(): lax.all_gather(up_weight[layer_idx], ('dp', 'shard'), axis=0, tiled=True)  75.5 us
    dot_general x4, matrix products, contract_first(): lax.dot_general(left, right, (((0,), (0,)), ((), ())), preferred_element_...  58 us
    all_gather x1, waiting for transfers between devices, shards(): lax.all_gather(attn_weight[layer_idx], ('dp', 'shard'), axis=0, tiled=True)  40.9 us
    dot_general x4, matrix products, contract_last(): lax.dot_general(left, right, (((1,), (1,)), ((), ())), preferred_element_...  23.5 us
  transfers between devices with their start and end apart: 6, of which 6 were waited for; matrix products, arithmetic and copies ran while one was open for 6% of the time, Pallas kernels for 0%

commit v1 on v0

--- a/solution.py
+++ b/solution.py
@@ -2,6 +2,7 @@
 import jax.numpy as jnp
 from jax import lax
 from jax.sharding import PartitionSpec as P
+from jax.lax import all_to_all, axis_size
 
 HEAD_DIM = 64
 EPS = 1e-05
@@ -216,10 +217,23 @@
     hidden = tokens.astype(jnp.float32)
     kept_params = []
     layer_idx = 0
+
+    def _pair_joints(incoming_x, row_dim):
+        num_devices = axis_size(("dp", "shard"))
+        pile = [num_devices if t == row_dim else 1 for t in range(incoming_x.ndim)]
+        even = all_to_all(
+            jnp.tile(incoming_x, pile),
+            axis_name=("dp", "shard"),
+            split_axis=row_dim,
+            concat_axis=row_dim,
+            tiled=True,
+        )
+        return even
+
     gathered = (
         lax.all_gather(attn_weight[layer_idx], ("dp", "shard"), axis=0, tiled=True),
         lax.all_gather(up_weight[layer_idx], ("dp", "shard"), axis=0, tiled=True),
-        lax.all_gather(down_weight[layer_idx], ("dp", "shard"), axis=0, tiled=True),
+        _pair_joints(down_weight[layer_idx], 0),
         lax.all_gather(vectors[layer_idx], ("dp", "shard"), axis=0, tiled=True),
     )
     kept_params.append(gathered)

time: 998 us -> 1120 us (1.12)
  blocking collectives: 84.6 us -> 371 us
  waiting for transfers between devices: 767 us -> 599 us
    unnamed x2, blocking collectives: 84.6 us -> 371 us
    unnamed x9, waiting for transfers between devices: 572 us -> 404 us
  transfers between devices with their start and end apart: 6 -> 7, of which waited for: 6 -> 5; matrix products, arithmetic and copies ran while one was open for 6% -> 6% of each run, Pallas kernels for 0% -> 0%
where the time goes in v1:
time: 1120 us; the launch traced here: 1110 us
  waiting for transfers between devices  599 us (53%)
  blocking collectives  371 us (33%)
  matrix products  107 us (10%)
  between operations  14.7 us (1%)
  local copies, waits for them, and re-layouts  11.4 us (1%)
    unnamed x9, waiting for transfers between devices  404 us
    unnamed x2, blocking collectives  371 us
    all_gather x1, waiting for transfers between devices, shards(): lax.all_gather(down_weight[layer_idx], ('dp', 'shard'), axis=0, tiled=True)  78.3 us
    all_gather x1, waiting for transfers between devices, shards(): lax.all_gather(up_weight[layer_idx], ('dp', 'shard'), axis=0, tiled=True)  74.8 us
    dot_general x4, matrix products, contract_first(): lax.dot_general(left, right, (((0,), (0,)), ((), ())), preferred_element_...  54.3 us
    all_gather x1, waiting for transfers between devices, shards(): lax.all_gather(attn_weight[layer_idx], ('dp', 'shard'), axis=0, tiled=True)  40.9 us
    dot_general x4, matrix products, contract_last(): lax.dot_general(left, right, (((1,), (1,)), ((), ())), preferred_element_...  22.7 us
  transfers between devices with their start and end apart: 7, of which 5 were waited for; matrix products, arithmetic and copies ran while one was open for 6% of the time, Pallas kernels for 0%

profile of v1, /device:TPU:0, one launch (start us, length us, event | category | flops | bytes accessed | tf_op | source)
XLA Modules:
  0.0 1113.8 jit_solution(16578234807698125536)
XLA Ops:
  7.2 0.7 all-gather.8.cloned.1.call-update
  7.9 0.7 all-gather.10.cloned.1.call-update
  8.7 0.7 all-gather.12.cloned.1.call-update
  9.4 0.7 reduce.3
  10.1 0.3 dynamic-update-slice
  10.4 43.7 %all-reduce = bf16[13056]{0:T(1024)(128)(2,1)S(1)} all-reduce(bf16[13056]{0:T(1024)(128)(2,1)S(1)} %dynamic-update-slice), channel_id=2, replica_groups=mesh['dp'=16,'shard'=2] {'dp','shard'}, use_global_device_ids=true, to_apply=%add | all-reduce | flops 13056 | bytes 52224
  54.2 0.7 convert_reduce_fusion.2
  55.1 1.1 convert_reduce_fusion
  56.2 1.1 fusion.45
  57.4 40.9 %all-gather.8.cloned.1.call-done = bf16[1,4352,1088]{2,1,0:T(8,128)(2,1)} async-done(((bf16[1,136,1088]{2,1,0:T(8,128)(2,1)}), bf16[1,4352,1088]{2,1,0:T(8,128)(2,1)}) %all-gather.8.cloned.1.call-update) | async-done | bytes 9469968 | tf_op jit(solution)/shard_map/all_gather | solution.py:234
  98.4 5.4 fusion.8
  103.9 0.4 fusion.48
  104.3 0.7 copy-done.8
  105.0 0.4 convolution_select_fusion
  105.3 0.5 convolution_convert_fusion.2
  105.8 3.0 fusion.85
  108.9 0.2 multiply_reduce_fusion.3
  109.0 74.8 %all-gather.10.cloned.1.call-done = bf16[1,4352,1088]{2,1,0:T(8,128)(2,1)} async-done(((bf16[1,136,1088]{2,1,0:T(8,128)(2,1)}), bf16[1,4352,1088]{2,1,0:T(8,128)(2,1)}) %all-gather.10.cloned.1.call-update) | async-done | bytes 9469968 | tf_op jit(solution)/shard_map/all_gather | solution.py:235
  183.8 7.2 fusion.9
  191.1 78.3 %all-gather.12.cloned.1.call-done = bf16[1,4352,1088]{2,1,0:T(8,128)(2,1)} async-done(((bf16[1,136,1088]{2,1,0:T(8,128)(2,1)}), bf16[1,4352,1088]{2,1,0:T(8,128)(2,1)}) %all-gather.12.cloned.1.call-update) | async-done | bytes 9469968 | tf_op jit(solution)/shard_map/all_gather | solution.py:249
  269.3 7.4 fusion.88
  276.8 4.7 multiply_reduce_fusion.1
  281.6 0.2 fusion.82
  281.9 0.8 copy-done.2
  282.7 0.7 copy-done.17
  283.4 2.6 convolution_convert_fusion
  286.1 0.4 fusion.89
  286.4 1.0 copy-done.6
  287.4 1.2 multiply_reduce_fusion
  288.7 0.2 multiply_convert_fusion.1
  288.9 0.8 copy-done.11
  289.6 0.4 fusion.84
  290.0 1.2 convolution_convert_fusion.1
  291.2 2.9 fusion.83
  294.1 11.0 fusion.26
  305.1 20.0 %convolution_add_fusion = f32[4352,1088]{1,0:T(8,128)} fusion(f32[4352,1088]{1,0:T(8,128)} %fusion.26, bf16[128,1088]{0,1:T(8,128)(2,1)S(1)} %copy-done.18, pred[4352]{0:T(1024)(128)(4,1)S(1)} %iota_compare_fusion.1, bf16[128,1088]{0,1:T(8,128)(2,1)S(1)} %bitcast.85, bf16[128,1088]{0,1:T(8,128)(2,1)S(1)} %bitcast.82, bf16[128,1088]{0,1:T(8,128)(2,1)S(1)} %bitcast.74, ...), kind=kOutput, calls=%fused_computation.1 | convolution fusion | flops 1221902336 | bytes 39276800 | tf_op jit(solution)/shard_map/dot_general | solution.py:33
  325.2 12.6 %fusion.52 = f32[4352,1088]{1,0:T(8,128)} fusion(bf16[128,4352]{1,0:T(8,128)(2,1)} %copy-done.4, f32[128,1088]{0,1:T(8,128)S(1)} %get-tuple-element.33, f32[1088]{0:T(1024)S(1)} %get-tuple-element.16, f32[1088]{0:T(1024)S(1)} %get-tuple-element.15, f32[128]{0:T(128)S(1)} %fusion.72, f32[128]{0:T(128)S(1)} %broadcast_multiply_fusion), kind=kOutput, calls=%fused_computation.80 | convolution fusion | flops 1212850176 | bytes 20620800 | tf_op jit(solution)/shard_map/dot_general | solution.py:33
  337.8 10.8 fusion.80
  348.6 6.1 tile.9
  354.7 4.0 all-to-all-start
  358.8 7.2 fusion.81
  366.0 0.4 fusion.44
  366.5 1.2 convert_reduce_fusion.1
  367.8 326.9 %all-reduce.4 = f32[13056]{0:T(1024)S(1)} all-reduce(f32[13056]{0:T(1024)S(1)} %concatenate.13), channel_id=9, replica_groups=mesh['dp'=16,'shard'=2] {'dp','shard'}, use_global_device_ids=true, to_apply=%region_23.24.clone | all-reduce | flops 13056 | bytes 104448
  694.7 0.7 dynamic-slice.3
  695.4 8.9 fusion.14
  704.3 182.4 %reduce-scatter.12.cloned.1.call-done = f32[136,1088]{1,0:T(8,128)} async-done(((f32[4352,1088]{1,0:T(8,128)}), f32[136,1088]{1,0:T(8,128)}) %reduce-scatter.12.cloned.1.call-update) | async-done | bytes 591888
  886.8 219.9 %reduce-scatter.14.cloned.1.call-done = f32[136,1088]{1,0:T(8,128)} async-done(((f32[4352,1088]{1,0:T(8,128)}), f32[136,1088]{1,0:T(8,128)}) %reduce-scatter.14.cloned.1.call-update) | async-done | bytes 591888
  (70 shorter events, 1.1 us)
Async XLA Ops:
  7.2 91.2 %all-gather.8.cloned.1.call-start = ((), (), s32[]{:S(2)}) async-start(), calls=%async_computation.4 | async-start | bytes 10340352 | tf_op jit(solution)/shard_map/all_gather | solution.py:234
  7.9 175.9 %all-gather.10.cloned.1.call-start = ((), (), s32[]{:S(2)}) async-start(), calls=%async_computation.5 | async-start | bytes 10340352 | tf_op jit(solution)/shard_map/all_gather | solution.py:235
  8.6 260.7 %all-gather.12.cloned.1.call-start = ((), (), s32[]{:S(2)}) async-start(), calls=%async_computation.6 | async-start | bytes 10340352 | tf_op jit(solution)/shard_map/all_gather | solution.py:249
  9.4 694.9 %reduce-scatter.10.cloned.1.call-start = ((), (), s32[]{:S(2)}) async-start(), calls=%async_computation.7 | async-start | bytes 20680704
  103.9 1.5 copy-start.10
  103.9 2.0 copy-start.1
  104.2 0.7 copy-start.8
  104.3 1.6 copy-start.19
  105.3 3.5 copy-start.5
  105.8 3.2 copy-start.15
  183.8 85.5 %copy-start.12 = (bf16[128,1088]{0,1:T(8,128)(2,1)S(1)}, bf16[128,1088]{0,1:T(8,128)(2,1)}, u32[]{:S(2)}) copy-start(bf16[128,1088]{0,1:T(8,128)(2,1)} %param.13) | copy-start | bytes 835588
  269.3 7.5 copy-start
  276.8 4.8 copy-start.4
  281.8 0.8 copy-start.2
  282.7 0.7 copy-start.17
  283.4 2.6 copy-start.20
  286.0 2.6 copy-start.21
  286.0 1.4 copy-start.6
  288.7 1.0 copy-start.11
  288.7 1.3 copy-start.9
  294.1 11.0 copy-start.7
  294.1 11.0 copy-start.14
  294.1 11.0 copy-start.16
  294.1 11.0 copy-start.18
  325.1 561.6 %reduce-scatter.12.cloned.1.call-start = ((), (), s32[]{:S(2)}) async-start(), calls=%async_computation.8 | async-start | bytes 20680704
  337.8 768.9 %reduce-scatter.14.cloned.1.call-start = ((), (), s32[]{:S(2)}) async-start(), calls=%async_computation.9 | async-start | bytes 20680704
  354.7 340.7 %all-to-all-start = ((bf16[32,136,1088]{2,1,0:T(8,128)(2,1)}), bf16[32,136,1088]{2,1,0:T(8,128)(2,1)}, u32[]{:S(2)}, u32[]{:S(2)}) async-start(bf16[32,136,1088]{2,1,0:T(8,128)(2,1)} %tile.9), calls=%async_computation | async-start | bytes 20054016 | tf_op jit(solution)/shard_map/all_to_all | solution.py:224
  358.8 7.7 copy-start.3
  358.8 7.7 copy-start.13
Sparse Core Ops, SparseCore 0:
  10.8 87.5 all-gather.7
  101.2 82.5 all-gather.9
  186.7 82.5 all-gather.11
  325.2 341.7 reduce-scatter.9
  673.9 212.7 reduce-scatter.11
  893.6 213.0 reduce-scatter.13
